TPU v7x, 32 devices: a whole 2x2x4 slice. The times are simulated.
32 devices in a mesh: slab: 8 (over z, y), subj: 2 (over core), tm: 2 (over x).
Axes of the slice: x: 2, y: 2, z: 4, core: 2. Of those that a mesh axis runs over, the one named last changes fastest.
Arguments:
- subject_data: bfloat16 [2, 16, 128, 2048], P('subj', 'slab', None, 'tm'), may hold values from -8 to 8
- template: bfloat16 [16, 128, 2048], P('slab', None, 'tm'), may hold values from -8 to 8
- neighbours: int32 [16, 27], P('slab'), may hold values from 0 to 15, as said below
- valid: int32 [16, 27], P('slab'), may hold values from 0 to 1, as said below
Outputs:
- new_template: bfloat16 [16, 128, 2048], P('slab', None, 'tm')
Inputs may be any that keep to these rules, and one draw needn't show every extreme that they name: `neighbours`: slots 9 l to 9 l + 8 of block b name blocks of the slab of b shifted by l - 1 (slabs hold 2 consecutive blocks); where that slab doesn't exist they name b itself. Slot 13 names b itself. `valid`: slot 13 is always 1; slots whose slab doesn't exist are 0.
All inputs are finite; a program needn't handle non-finite values.
Results may differ from a plain program's by a relative error of at most 0.007.
Values may be sent and summed in bfloat16 or wider, within the bound.
No kernel may reach another device: no remote copies, remote signals or barrier semaphores. Data moves between devices by JAX's collectives and lax.ppermute only.
A program may use at most 64 MiB of HBM per device.

v0:
```python
import jax
import jax.numpy as jnp
from jax import lax
from jax.sharding import PartitionSpec as P

ITERS = 3


def with_halo(cells, sides, width):
    for axis, dim in sides:
        count = lax.axis_size(axis)
        ends = count - 1
        head = lax.slice_in_dim(cells, 0, width, axis=dim)
        tail = lax.slice_in_dim(cells, cells.shape[dim] - width, cells.shape[dim], axis=dim)
        cells = jnp.concatenate(
            [
                lax.ppermute(tail, axis, [(i, (i + 1) % count) for i in range(ends)]),
                cells,
                lax.ppermute(head, axis, [((i + 1) % count, i) for i in range(ends)]),
            ],
            axis=dim,
        )
    return cells


def balance(cross, row_norm, col_norm, mask):
    width = cross.shape[-1]
    logits = cross * row_norm[None, :, None, None] * col_norm[:, None, :, :] / 0.03
    masked = mask[None, None, :, None]
    kernel = jnp.exp(logits) * masked
    target = masked / (width * jnp.sum(mask))
    filler = 1.0 - masked
    col_weight = jnp.ones((cross.shape[0], 1, cross.shape[2], width), jnp.float32)
    for step in range(ITERS):
        row_weight = 1.0 / width / jnp.sum(kernel * col_weight, axis=(2, 3), keepdims=True)
        col_weight = target / (jnp.sum(kernel * row_weight, axis=1, keepdims=True) + filler)
    flow = kernel * col_weight
    return (flow / jnp.sum(flow, axis=(2, 3), keepdims=True)).astype(jnp.bfloat16)


def square_sum(values):
    return jnp.einsum("...t,...t->...", values, values, preferred_element_type=jnp.float32)


def slot_cross(tmpl_block, extended, slots):
    whole = jnp.einsum("it,sejt->siej", tmpl_block, extended, preferred_element_type=jnp.float32)
    return jnp.take(whole, slots, axis=2)


def project(plan, extended, slots):
    places = (slots[:, None] == jnp.arange(extended.shape[1], dtype=jnp.int32)[None, :]).astype(
        jnp.float32
    )
    folded = jnp.einsum(
        "sikj,ke->siej", plan.astype(jnp.float32), places, precision=lax.Precision.HIGHEST
    )
    upper = folded.astype(jnp.bfloat16)
    lower = (folded - upper.astype(jnp.float32)).astype(jnp.bfloat16)
    total = jnp.einsum("siej,sejt->it", upper, extended, preferred_element_type=jnp.float32)
    return total + jnp.einsum("siej,sejt->it", lower, extended, preferred_element_type=jnp.float32)


def subject_mean(moved, count):
    total = lax.psum(moved, "subj")
    return (total / count).astype(jnp.bfloat16)


def on_device(subject_data, template, neighbours, valid):
    blocks_here = template.shape[0]
    share = blocks_here // lax.axis_size("tm")
    subjects_all = subject_data.shape[0] * lax.axis_size("subj")
    offsets = neighbours - (lax.axis_index("slab") - 1) * blocks_here
    mask_all = valid.astype(jnp.float32)
    first = lax.axis_index("tm") * share
    my_offsets = lax.dynamic_slice_in_dim(offsets, first, share, 0)
    my_mask = lax.dynamic_slice_in_dim(mask_all, first, share, 0)
    full_time = lax.all_gather(subject_data, "tm", axis=3, tiled=True)
    extended = with_halo(full_time, (("slab", 1),), blocks_here)
    mine = lax.all_to_all(template, "tm", split_axis=0, concat_axis=2, tiled=True)
    col_norm = lax.rsqrt(square_sum(extended) + 1e-06)
    row_norm = lax.rsqrt(square_sum(mine) + 1e-06)

    def one_block(inputs):
        tmpl_block, scale_rows, slots, mask = inputs
        cross = slot_cross(tmpl_block, extended, slots)
        plan = balance(cross, scale_rows, jnp.take(col_norm, slots, axis=1), mask)
        return project(plan, extended, slots)

    moved = lax.map(one_block, (mine, row_norm, my_offsets, my_mask))
    averaged = subject_mean(moved, subjects_all)
    return lax.all_to_all(averaged, "tm", split_axis=2, concat_axis=0, tiled=True)


def solution(mesh):
    placed = (
        P("subj", "slab", None, "tm"),
        P("slab", None, "tm"),
        P("slab", None),
        P("slab", None),
    )
    return jax.shard_map(
        on_device, mesh=mesh, in_specs=placed, out_specs=P("slab", None, "tm"), check_vma=False
    )
```

profile of v0, /device:TPU:0, one launch (start us, length us, event | category | flops | bytes accessed | tf_op | source)
XLA Modules:
  0.0 159.5 jit_solution(255287246146315666)
XLA Ops:
  7.3 4.2 %all-to-all-start = ((bf16[2,128,1024]{2,1,0:T(8,128)(2,1)}), bf16[2,128,1024]{2,1,0:T(8,128)(2,1)S(1)}, u32[]{:S(2)}, u32[]{:S(2)}) async-start(bf16[2,128,1024]{2,1,0:T(8,128)(2,1)} %param.5), calls=%async_computation | async-start | bytes 1048576 | tf_op jit(solution)/shard_map/all_to_all | solution.py:79
  11.5 21.4 %all-gather.2.cloned.1.call-done = bf16[1,2,128,2048]{3,2,1,0:T(8,128)(2,1)} async-done(((bf16[1,2,128,1024]{3,2,1,0:T(8,128)(2,1)}), bf16[1,2,128,2048]{3,2,1,0:T(8,128)(2,1)}) %all-gather.2.cloned.1.call-update) | async-done | bytes 1048592 | tf_op jit(solution)/shard_map/all_gather | solution.py:77
  32.9 1.3 collective-permute-start.1
  34.2 5.5 %collective-permute-start = (bf16[1,2,128,2048]{3,2,1,0:T(8,128)(2,1)}, bf16[1,2,128,2048]{3,2,1,0:T(8,128)(2,1)}, u32[]{:S(2)}, u32[]{:S(2)}) collective-permute-start(bf16[1,2,128,2048]{3,2,1,0:T(8,128)(2,1)} %all-gather.2.cloned.1.call-done), channel_id=1, source_target_pairs={{0,4},{4,8},{8,12},{12,16},{16,20},{20,24},{24,28},{1,5},{5,9},{9,... | collective-permute-start | bytes 3145736 | tf_op jit(solution)/shard_map/ppermute | solution.py:17
  43.0 1.2 reshape.327
  44.5 15.2 %collective-permute-done.1 = bf16[1,2,128,2048]{3,2,1,0:T(8,128)(2,1)S(1)} collective-permute-done((bf16[1,2,128,2048]{3,2,1,0:T(8,128)(2,1)}, bf16[1,2,128,2048]{3,2,1,0:T(8,128)(2,1)S(1)}, u32[]{:S(2)}, u32[]{:S(2)}) %collective-permute-start.1) | collective-permute-done | bytes 1048608 | tf_op jit(solution)/shard_map/ppermute | solution.py:19
  59.7 22.5 %collective-permute-done = bf16[1,2,128,2048]{3,2,1,0:T(8,128)(2,1)} collective-permute-done((bf16[1,2,128,2048]{3,2,1,0:T(8,128)(2,1)}, bf16[1,2,128,2048]{3,2,1,0:T(8,128)(2,1)}, u32[]{:S(2)}, u32[]{:S(2)}) %collective-permute-start) | collective-permute-done | bytes 1048608 | tf_op jit(solution)/shard_map/ppermute | solution.py:17
  82.2 1.8 %fusion = f32[6,128]{1,0:T(8,128)S(1)} fusion(bf16[1,2,128,2048]{3,2,1,0:T(8,128)(2,1)S(1)} %collective-permute-done.1, bf16[1,2,128,2048]{3,2,1,0:T(8,128)(2,1)S(1)} %copy-done, bf16[1,2,128,2048]{3,2,1,0:T(8,128)(2,1)} %collective-permute-done), kind=kLoop, calls=%fused_computation.3 | loop fusion | flops 7863552 | bytes 3148800 | tf_op jit(solution)/shard_map/...t,...t->.../dot_general | solution.py:42
  84.6 2.3 %convolution_bitcast_fusion.3 = f32[128,6,128]{0,2,1:T(8,128)S(1)} fusion(bf16[128,2048,1]{1,0,2:T(8,128)(2,1)} %reshape.327, bf16[1,2,128,2048]{3,2,1,0:T(8,128)(2,1)S(1)} %collective-permute-done.1, bf16[1,2,128,2048]{3,2,1,0:T(8,128)(2,1)S(1)} %copy-done, bf16[1,2,128,2048]{3,2,1,0:T(8,128)(2,1)} %collective-permute-done), kind=kOutput, calls=%fused_computation.31 | convolution fusion | flops 405798912 | bytes 4063232 | tf_op jit(solution)/shard_map/while/body/eval_jaxpr/it,sejt->siej/dot_general | solution.py:46
  88.5 1.4 multiply_reduce_fusion.5
  90.0 1.3 multiply_reduce_fusion.4
  91.3 1.4 multiply_reduce_fusion.3
  92.8 1.3 multiply_reduce_fusion.2
  94.1 1.4 multiply_reduce_fusion.1
  95.6 1.3 multiply_reduce_fusion
  96.9 1.3 fusion.15
  98.3 1.3 copy.17
  99.9 2.8 %convolution_bitcast_fusion = f32[128,2048]{1,0:T(8,128)S(1)} fusion(bf16[128,6,128]{2,1,0:T(8,128)(2,1)S(1)} %get-tuple-element.32, bf16[1,2,128,2048]{3,2,1,0:T(8,128)(2,1)} %copy-done.2, bf16[1,2,128,2048]{3,2,1,0:T(8,128)(2,1)} %all-gather.2.cloned.1.call-done, bf16[1,2,128,2048]{3,2,1,0:T(8,128)(2,1)} %collective-permute-done), kind=kOutput, calls=%fused_computation.5 | convolution fusion | flops 405798912 | bytes 4390912 | tf_op jit(solution)/shard_map/while/body/eval_jaxpr/siej,sejt->it/dot_general | solution.py:60
  102.7 3.0 %fusion.2 = f32[1,128,2048]{2,1,0:T(8,128)} fusion(f32[128,2048]{1,0:T(8,128)S(1)} %convolution_bitcast_fusion, bf16[128,6,128]{2,1,0:T(8,128)(2,1)S(1)} %get-tuple-element.23, bf16[1,2,128,2048]{3,2,1,0:T(8,128)(2,1)S(1)} %copy-done.3, bf16[1,2,128,2048]{3,2,1,0:T(8,128)(2,1)S(1)} %copy-done.1, bf16[1,2,128,2048]{3,2,1,0:T(8,128)(2,1)} %collective-permute-done), kind=kOutput, calls=%fused_computation.8 | convolution fusion | flops 406061056 | bytes 5439488 | tf_op jit(solution)/shard_map/while/body/eval_jaxpr/siej,sejt->it/dot_general | solution.py:59
  105.7 19.7 %all-reduce.2.cloned.1.call-done = f32[1,128,2048]{2,1,0:T(8,128)} async-done(((f32[1,128,2048]{2,1,0:T(8,128)}), f32[1,128,2048]{2,1,0:T(8,128)}) %all-reduce.2.cloned.1.call-update) | async-done | bytes 1048592 | tf_op jit(solution)/shard_map/psum | solution.py:64
  125.4 1.3 multiply_convert_fusion
  128.0 11.7 %reduce.12 = bf16[2048,128]{1,0:T(8,128)(2,1)S(1)} reduce(bf16[2048,1,128]{2,1,0:T(2,128)(2,1)S(1)} %bitcast.110, bf16[]{:T(256)} %broadcast.450), dimensions={1}, to_apply=%bitcast.98.reduce_sub_computation | reduce | bytes 1048578
  139.9 11.2 %all_to_all.33 = bf16[2,2,65536]{2,1,0:T(2,128)(2,1)S(1)} all-to-all(bf16[2,2,65536]{2,1,0:T(2,128)(2,1)S(1)} %reshape.335), channel_id=1, replica_groups=mesh['slab'=8,'subj'=2,'tm'=2] {'tm'}, dimensions={0} | all-to-all | bytes 1048576 | tf_op jit(solution)/shard_map/all_to_all | solution.py:91
  151.7 1.0 copy.21
  (42 shorter events, 8.2 us)
Async XLA Ops:
  6.5 26.4 %all-gather.2.cloned.1.call-start = ((), (), s32[]{:S(2)}) async-start(), calls=%async_computation.2 | async-start | bytes 1572864 | tf_op jit(solution)/shard_map/all_gather | solution.py:77
  7.3 35.2 %all-to-all-start = ((bf16[2,128,1024]{2,1,0:T(8,128)(2,1)}), bf16[2,128,1024]{2,1,0:T(8,128)(2,1)S(1)}, u32[]{:S(2)}, u32[]{:S(2)}) async-start(bf16[2,128,1024]{2,1,0:T(8,128)(2,1)} %param.5), calls=%async_computation | async-start | bytes 1048576 | tf_op jit(solution)/shard_map/all_to_all | solution.py:79
  11.5 113.9 %all-reduce.2.cloned.1.call-start = ((), (), s32[]{:S(2)}) async-start(), calls=%async_computation.3 | async-start | bytes 2097152 | tf_op jit(solution)/shard_map/psum | solution.py:64
  32.9 26.8 %collective-permute-start.1 = (bf16[1,2,128,2048]{3,2,1,0:T(8,128)(2,1)}, bf16[1,2,128,2048]{3,2,1,0:T(8,128)(2,1)S(1)}, u32[]{:S(2)}, u32[]{:S(2)}) collective-permute-start(bf16[1,2,128,2048]{3,2,1,0:T(8,128)(2,1)} %all-gather.2.cloned.1.call-done), channel_id=1, source_target_pairs={{4,0},{8,4},{12,8},{16,12},{20,16},{24,20},{28,24},{5,1},{9,5},{13... | collective-permute-start | bytes 3145736 | tf_op jit(solution)/shard_map/ppermute | solution.py:19
  34.2 48.0 %collective-permute-start = (bf16[1,2,128,2048]{3,2,1,0:T(8,128)(2,1)}, bf16[1,2,128,2048]{3,2,1,0:T(8,128)(2,1)}, u32[]{:S(2)}, u32[]{:S(2)}) collective-permute-start(bf16[1,2,128,2048]{3,2,1,0:T(8,128)(2,1)} %all-gather.2.cloned.1.call-done), channel_id=1, source_target_pairs={{0,4},{4,8},{8,12},{12,16},{16,20},{20,24},{24,28},{1,5},{5,9},{9,... | collective-permute-start | bytes 3145736 | tf_op jit(solution)/shard_map/ppermute | solution.py:17
  42.5 39.7 %copy-start = (bf16[1,2,128,2048]{3,2,1,0:T(8,128)(2,1)S(1)}, bf16[1,2,128,2048]{3,2,1,0:T(8,128)(2,1)}, u32[]{:S(2)}) copy-start(bf16[1,2,128,2048]{3,2,1,0:T(8,128)(2,1)} %all-gather.2.cloned.1.call-done) | copy-start | bytes 3145732
  59.7 27.2 %copy-start.2 = (bf16[1,2,128,2048]{3,2,1,0:T(8,128)(2,1)}, bf16[1,2,128,2048]{3,2,1,0:T(8,128)(2,1)S(1)}, u32[]{:S(2)}) copy-start(bf16[1,2,128,2048]{3,2,1,0:T(8,128)(2,1)S(1)} %collective-permute-done.1) | copy-start | bytes 3145732
  99.9 2.8 %copy-start.1 = (bf16[1,2,128,2048]{3,2,1,0:T(8,128)(2,1)S(1)}, bf16[1,2,128,2048]{3,2,1,0:T(8,128)(2,1)}, u32[]{:S(2)}) copy-start(bf16[1,2,128,2048]{3,2,1,0:T(8,128)(2,1)} %all-gather.2.cloned.1.call-done) | copy-start | bytes 3145732
  99.9 2.8 %copy-start.3 = (bf16[1,2,128,2048]{3,2,1,0:T(8,128)(2,1)S(1)}, bf16[1,2,128,2048]{3,2,1,0:T(8,128)(2,1)}, u32[]{:S(2)}) copy-start(bf16[1,2,128,2048]{3,2,1,0:T(8,128)(2,1)} %copy-done.2) | copy-start | bytes 3145732
Sparse Core Ops, SparseCore 0:
  8.9 23.9 all-gather.1
  105.8 19.5 all-reduce.1
where the time goes:
time: 160 us
  waiting for transfers between devices  79.5 us (50%)
  other arithmetic  27.6 us (17%)
  between operations  14.3 us (9%)
  blocking collectives  11.2 us (7%)
  starting transfers between devices  11.1 us (7%)
  matrix products  8.34 us (5%)
  local copies, waits for them, and re-layouts  7.44 us (5%)
    ppermute x1, waiting for transfers between devices, with_halo(): lax.ppermute(tail, axis, [(i, (i + 1) % count) for i in range(ends)])  22.5 us
    all_gather x1, waiting for transfers between devices, on_device(): full_time = lax.all_gather(subject_data, 'tm', axis=3, tiled=True)  21.4 us
    psum x1, waiting for transfers between devices, subject_mean(): total = lax.psum(moved, 'subj')  19.7 us
    ppermute x1, waiting for transfers between devices, with_halo(): lax.ppermute(head, axis, [((i + 1) % count, i) for i in range(ends)])  15.2 us
    unnamed x1, other arithmetic  11.7 us
    all_to_all x1, blocking collectives, on_device(): lax.all_to_all(averaged, 'tm', split_axis=2, concat_axis=0, tiled=True)  11.2 us
    ppermute x1, starting transfers between devices, with_halo(): lax.ppermute(tail, axis, [(i, (i + 1) % count) for i in range(ends)])  5.54 us
    all_to_all x1, starting transfers between devices, on_device(): lax.all_to_all(template, 'tm', split_axis=0, concat_axis=2, tiled=True)  4.25 us
  transfers between devices with their start and end apart: 5, of which 4 were waited for; matrix products, arithmetic and copies ran while one was open for 3% of the time, Pallas kernels for 0%

commit v1 on v0

--- a/solution.py
+++ b/solution.py
@@ -4,6 +4,18 @@
 from jax.sharding import PartitionSpec as P
 
 ITERS = 3
+
+
+def doubled_up(shard, axis, dim):
+    ways, here = (lax.axis_size(axis), lax.axis_index(axis))
+    grown, reach = (shard, 1)
+    while reach < ways:
+        theirs = lax.ppermute(grown, axis, [(d, d ^ reach) for d in range(ways)])
+        mine_first = jnp.concatenate([grown, theirs], axis=dim)
+        theirs_first = jnp.concatenate([theirs, grown], axis=dim)
+        grown = jnp.where(here & reach == 0, mine_first, theirs_first)
+        reach = 2 * reach
+    return grown
 
 
 def with_halo(cells, sides, width):
@@ -74,7 +86,7 @@
     first = lax.axis_index("tm") * share
     my_offsets = lax.dynamic_slice_in_dim(offsets, first, share, 0)
     my_mask = lax.dynamic_slice_in_dim(mask_all, first, share, 0)
-    full_time = lax.all_gather(subject_data, "tm", axis=3, tiled=True)
+    full_time = doubled_up(subject_data, "tm", 3)
     extended = with_halo(full_time, (("slab", 1),), blocks_here)
     mine = lax.all_to_all(template, "tm", split_axis=0, concat_axis=2, tiled=True)
     col_norm = lax.rsqrt(square_sum(extended) + 1e-06)

time: 160 us -> 152 us (0.950)
  waiting for transfers between devices: 79.5 us -> 67.8 us
  starting transfers between devices: 11.1 us -> 13.4 us
    all_gather x1 -> x0, waiting for transfers between devices: 21.4 us -> none  [on_device(): full_time = lax.all_gather(subject_data, 'tm', axis=3, tiled=True)]
    ppermute x0 -> x1, waiting for transfers between devices: none -> 9.43 us  [doubled_up(): theirs = lax.ppermute(grown, axis, [(d, d ^ reach) for d in range(ways)])]
    ppermute x0 -> x1, starting transfers between devices: none -> 2.97 us  [doubled_up(): theirs = lax.ppermute(grown, axis, [(d, d ^ reach) for d in range(ways)])]
    select_n x0 -> x1, other arithmetic: none -> 1.69 us  [doubled_up(): grown = jnp.where(here & reach == 0, mine_first, theirs_first)]
where the time goes in v1:
time: 152 us
  waiting for transfers between devices  67.8 us (45%)
  other arithmetic  28.9 us (19%)
  between operations  14.3 us (9%)
  starting transfers between devices  13.4 us (9%)
  blocking collectives  11.2 us (7%)
  local copies, waits for them, and re-layouts  8.1 us (5%)
  matrix products  7.86 us (5%)
    ppermute x1, waiting for transfers between devices, with_halo(): lax.ppermute(tail, axis, [(i, (i + 1) % count) for i in range(ends)])  22.4 us
    psum x1, waiting for transfers between devices, subject_mean(): total = lax.psum(moved, 'subj')  20.9 us
    ppermute x1, waiting for transfers between devices, with_halo(): lax.ppermute(head, axis, [((i + 1) % count, i) for i in range(ends)])  15.1 us
    unnamed x1, other arithmetic  11.7 us
    all_to_all x1, blocking collectives, on_device(): lax.all_to_all(averaged, 'tm', split_axis=2, concat_axis=0, tiled=True)  11.2 us
    ppermute x1, waiting for transfers between devices, doubled_up(): theirs = lax.ppermute(grown, axis, [(d, d ^ reach) for d in range(ways)])  9.43 us
    ppermute x1, starting transfers between devices, with_halo(): lax.ppermute(tail, axis, [(i, (i + 1) % count) for i in range(ends)])  5.58 us
    reduce_sum x3, other arithmetic, balance(): jnp.sum(kernel * row_weight, axis=1, keepdims=True) + filler  4.12 us
  transfers between devices with their start and end apart: 5, of which 4 were waited for; matrix products, arithmetic and copies ran while one was open for 3% of the time, Pallas kernels for 0%

profile of v1, /device:TPU:0, one launch (start us, length us, event | category | flops | bytes accessed | tf_op | source)
XLA Modules:
  0.0 151.6 jit_solution(15554880157844449094)
XLA Ops:
  6.5 3.0 %collective-permute-start = (bf16[1,2,128,1024]{3,2,1,0:T(8,128)(2,1)}, bf16[1,2,128,1024]{3,2,1,0:T(8,128)(2,1)S(1)}, u32[]{:S(2)}, u32[]{:S(2)}) collective-permute-start(bf16[1,2,128,1024]{3,2,1,0:T(8,128)(2,1)} %param.4), channel_id=1, source_target_pairs={{0,1},{1,0},{2,3},{3,2},{4,5},{5,4},{6,7},{7,6},{8,9},{9,8},{10,11... | collective-permute-start | bytes 1572872 | tf_op jit(solution)/shard_map/ppermute | solution.py:13
  9.5 3.5 %all-to-all-start = ((bf16[2,128,1024]{2,1,0:T(8,128)(2,1)}), bf16[2,128,1024]{2,1,0:T(8,128)(2,1)S(1)}, u32[]{:S(2)}, u32[]{:S(2)}) async-start(bf16[2,128,1024]{2,1,0:T(8,128)(2,1)} %param.5), calls=%async_computation | async-start | bytes 1048576 | tf_op jit(solution)/shard_map/all_to_all | solution.py:91
  13.1 9.4 %collective-permute-done = bf16[1,2,128,1024]{3,2,1,0:T(8,128)(2,1)S(1)} collective-permute-done((bf16[1,2,128,1024]{3,2,1,0:T(8,128)(2,1)}, bf16[1,2,128,1024]{3,2,1,0:T(8,128)(2,1)S(1)}, u32[]{:S(2)}, u32[]{:S(2)}) %collective-permute-start) | collective-permute-done | bytes 524320 | tf_op jit(solution)/shard_map/ppermute | solution.py:13
  22.5 1.7 %maximum_select_fusion = bf16[1,2,128,2048]{3,2,1,0:T(8,128)(2,1)S(1)} fusion(bf16[1,2,128,1024]{3,2,1,0:T(8,128)(2,1)S(1)} %collective-permute-done, bf16[1,2,128,1024]{3,2,1,0:T(8,128)(2,1)} %param.4, pred[]{:T(512)S(6)} %eq.29), kind=kLoop, calls=%fused_computation.32 | loop fusion | flops 4718592 | bytes 2097153 | tf_op jit(solution)/shard_map/jit(_where)/select_n | solution.py:16
  24.2 1.3 collective-permute-start.2
  25.5 5.6 %collective-permute-start.1 = (bf16[1,2,128,2048]{3,2,1,0:T(8,128)(2,1)S(1)}, bf16[1,2,128,2048]{3,2,1,0:T(8,128)(2,1)}, u32[]{:S(2)}, u32[]{:S(2)}) collective-permute-start(bf16[1,2,128,2048]{3,2,1,0:T(8,128)(2,1)S(1)} %maximum_select_fusion), channel_id=1, source_target_pairs={{0,4},{4,8},{8,12},{12,16},{16,20},{20,24},{24,28},{1,5},{5,9},{9,... | collective-permute-start | bytes 3145736 | tf_op jit(solution)/shard_map/ppermute | solution.py:29
  34.5 15.1 %collective-permute-done.2 = bf16[1,2,128,2048]{3,2,1,0:T(8,128)(2,1)S(1)} collective-permute-done((bf16[1,2,128,2048]{3,2,1,0:T(8,128)(2,1)S(1)}, bf16[1,2,128,2048]{3,2,1,0:T(8,128)(2,1)S(1)}, u32[]{:S(2)}, u32[]{:S(2)}) %collective-permute-start.2) | collective-permute-done | bytes 1048608 | tf_op jit(solution)/shard_map/ppermute | solution.py:31
  49.6 22.4 %collective-permute-done.1 = bf16[1,2,128,2048]{3,2,1,0:T(8,128)(2,1)} collective-permute-done((bf16[1,2,128,2048]{3,2,1,0:T(8,128)(2,1)S(1)}, bf16[1,2,128,2048]{3,2,1,0:T(8,128)(2,1)}, u32[]{:S(2)}, u32[]{:S(2)}) %collective-permute-start.1) | collective-permute-done | bytes 1048608 | tf_op jit(solution)/shard_map/ppermute | solution.py:29
  71.9 1.8 %fusion = f32[6,128]{1,0:T(8,128)S(1)} fusion(bf16[1,2,128,2048]{3,2,1,0:T(8,128)(2,1)S(1)} %collective-permute-done.2, bf16[1,2,128,2048]{3,2,1,0:T(8,128)(2,1)S(1)} %maximum_select_fusion, bf16[1,2,128,2048]{3,2,1,0:T(8,128)(2,1)} %collective-permute-done.1), kind=kLoop, calls=%fused_computation.3 | loop fusion | flops 7863552 | bytes 3148800 | tf_op jit(solution)/shard_map/...t,...t->.../dot_general | solution.py:54
  74.3 2.7 %convolution_bitcast_fusion.3 = f32[128,6,128]{0,2,1:T(8,128)S(1)} fusion(bf16[128,2048,1]{1,0,2:T(8,128)(2,1)} %reshape.379, bf16[1,2,128,2048]{3,2,1,0:T(8,128)(2,1)} %copy-done, bf16[1,2,128,2048]{3,2,1,0:T(8,128)(2,1)S(1)} %maximum_select_fusion, bf16[1,2,128,2048]{3,2,1,0:T(8,128)(2,1)} %collective-permute-done.1), kind=kOutput, calls=%fused_computation.31 | convolution fusion | flops 405798912 | bytes 4063232 | tf_op jit(solution)/shard_map/while/body/eval_jaxpr/it,sejt->siej/dot_general | solution.py:58
  78.6 1.4 multiply_reduce_fusion.5
  80.0 1.3 multiply_reduce_fusion.4
  81.4 1.4 multiply_reduce_fusion.3
  82.8 1.3 multiply_reduce_fusion.2
  84.2 1.4 multiply_reduce_fusion.1
  85.6 1.3 multiply_reduce_fusion
  87.0 2.3 %fusion.15 = bf16[128,27,128]{0,2,1:T(8,128)(2,1)} fusion(f32[27,128,128]{1,2,0:T(8,128)S(1)} %gather_fusion, f32[128]{0:T(128)S(1)} %multiply_reduce_fusion, f32[27,128]{1,0:T(8,128)S(1)} %add_divide_fusion, f32[27]{0:T(128)S(1)} %get-tuple-element.20, f32[27,128]{1,0:T(8,128)S(1)} %broadcast_select_fusion, f32[128]{0:T(128)S(1)} %add_rsqrt_fusion.1, ...), kind=kLoop, calls=%fused_computation.29 | loop fusion | flops 3538944 | bytes 2683015 | tf_op jit(solution)/shard_map/while/body/eval_jaxpr/convert_element_type | solution.py:50
  89.3 2.0 %copy.17 = bf16[128,27,128]{2,1,0:T(8,128)(2,1)S(1)} copy(bf16[128,27,128]{0,2,1:T(8,128)(2,1)} %fusion.15) | data formatting | bytes 1769472 | tf_op jit(solution)/shard_map/while/body/eval_jaxpr/convert_element_type | solution.py:50
  91.6 2.0 %convolution_bitcast_fusion = f32[128,2048]{1,0:T(8,128)S(1)} fusion(bf16[128,6,128]{2,1,0:T(8,128)(2,1)S(1)} %get-tuple-element.32, bf16[1,2,128,2048]{3,2,1,0:T(8,128)(2,1)S(1)} %copy-done.1, bf16[1,2,128,2048]{3,2,1,0:T(8,128)(2,1)S(1)} %maximum_select_fusion, bf16[1,2,128,2048]{3,2,1,0:T(8,128)(2,1)} %collective-permute-done.1), kind=kOutput, calls=%fused_computation.5 | convolution fusion | flops 405798912 | bytes 4390912 | tf_op jit(solution)/shard_map/while/body/eval_jaxpr/siej,sejt->it/dot_general | solution.py:72
  93.6 3.0 %fusion.2 = f32[1,128,2048]{2,1,0:T(8,128)} fusion(f32[128,2048]{1,0:T(8,128)S(1)} %convolution_bitcast_fusion, bf16[128,6,128]{2,1,0:T(8,128)(2,1)S(1)} %get-tuple-element.23, bf16[1,2,128,2048]{3,2,1,0:T(8,128)(2,1)S(1)} %copy-done.1, bf16[1,2,128,2048]{3,2,1,0:T(8,128)(2,1)S(1)} %maximum_select_fusion, bf16[1,2,128,2048]{3,2,1,0:T(8,128)(2,1)} %collective-permute-done.1), kind=kOutput, calls=%fused_computation.8 | convolution fusion | flops 406061056 | bytes 5439488 | tf_op jit(solution)/shard_map/while/body/eval_jaxpr/siej,sejt->it/dot_general | solution.py:71
  96.6 20.9 %all-reduce.2.cloned.1.call-done = f32[1,128,2048]{2,1,0:T(8,128)} async-done(((f32[1,128,2048]{2,1,0:T(8,128)}), f32[1,128,2048]{2,1,0:T(8,128)}) %all-reduce.2.cloned.1.call-update) | async-done | bytes 1048592 | tf_op jit(solution)/shard_map/psum | solution.py:76
  117.5 1.3 multiply_convert_fusion
  120.1 11.7 %reduce.12 = bf16[2048,128]{1,0:T(8,128)(2,1)S(1)} reduce(bf16[2048,1,128]{2,1,0:T(2,128)(2,1)S(1)} %bitcast.110, bf16[]{:T(256)} %broadcast.458), dimensions={1}, to_apply=%bitcast.98.reduce_sub_computation | reduce | bytes 1048578
  132.0 11.2 %all_to_all.33 = bf16[2,2,65536]{2,1,0:T(2,128)(2,1)S(1)} all-to-all(bf16[2,2,65536]{2,1,0:T(2,128)(2,1)S(1)} %reshape.387), channel_id=1, replica_groups=mesh['slab'=8,'subj'=2,'tm'=2] {'tm'}, dimensions={0} | all-to-all | bytes 1048576 | tf_op jit(solution)/shard_map/all_to_all | solution.py:103
  (42 shorter events, 8.4 us)
Async XLA Ops:
  6.5 24.5 %copy-start.2 = (s32[2,27]{1,0:T(2,128)S(1)}, s32[2,27]{1,0:T(2,128)}, u32[]{:S(2)}) copy-start(s32[2,27]{1,0:T(2,128)} %param.6) | copy-start | bytes 652
  6.5 24.5 %copy-start.3 = (s32[2,27]{1,0:T(2,128)S(1)}, s32[2,27]{1,0:T(2,128)}, u32[]{:S(2)}) copy-start(s32[2,27]{1,0:T(2,128)} %param.7) | copy-start | bytes 652
  6.5 15.9 %collective-permute-start = (bf16[1,2,128,1024]{3,2,1,0:T(8,128)(2,1)}, bf16[1,2,128,1024]{3,2,1,0:T(8,128)(2,1)S(1)}, u32[]{:S(2)}, u32[]{:S(2)}) collective-permute-start(bf16[1,2,128,1024]{3,2,1,0:T(8,128)(2,1)} %param.4), channel_id=1, source_target_pairs={{0,1},{1,0},{2,3},{3,2},{4,5},{5,4},{6,7},{7,6},{8,9},{9,8},{10,11... | collective-permute-start | bytes 1572872 | tf_op jit(solution)/shard_map/ppermute | solution.py:13
  9.5 22.9 %all-to-all-start = ((bf16[2,128,1024]{2,1,0:T(8,128)(2,1)}), bf16[2,128,1024]{2,1,0:T(8,128)(2,1)S(1)}, u32[]{:S(2)}, u32[]{:S(2)}) async-start(bf16[2,128,1024]{2,1,0:T(8,128)(2,1)} %param.5), calls=%async_computation | async-start | bytes 1048576 | tf_op jit(solution)/shard_map/all_to_all | solution.py:91
  13.0 104.5 %all-reduce.2.cloned.1.call-start = ((), (), s32[]{:S(2)}) async-start(), calls=%async_computation.2 | async-start | bytes 2097152 | tf_op jit(solution)/shard_map/psum | solution.py:76
  24.2 25.4 %collective-permute-start.2 = (bf16[1,2,128,2048]{3,2,1,0:T(8,128)(2,1)S(1)}, bf16[1,2,128,2048]{3,2,1,0:T(8,128)(2,1)S(1)}, u32[]{:S(2)}, u32[]{:S(2)}) collective-permute-start(bf16[1,2,128,2048]{3,2,1,0:T(8,128)(2,1)S(1)} %maximum_select_fusion), channel_id=1, source_target_pairs={{4,0},{8,4},{12,8},{16,12},{20,16},{24,20},{28,24},{5,1},{9,5},{13... | collective-permute-start | bytes 3145736 | tf_op jit(solution)/shard_map/ppermute | solution.py:31
  25.5 46.4 %collective-permute-start.1 = (bf16[1,2,128,2048]{3,2,1,0:T(8,128)(2,1)S(1)}, bf16[1,2,128,2048]{3,2,1,0:T(8,128)(2,1)}, u32[]{:S(2)}, u32[]{:S(2)}) collective-permute-start(bf16[1,2,128,2048]{3,2,1,0:T(8,128)(2,1)S(1)} %maximum_select_fusion), channel_id=1, source_target_pairs={{0,4},{4,8},{8,12},{12,16},{16,20},{20,24},{24,28},{1,5},{5,9},{9,... | collective-permute-start | bytes 3145736 | tf_op jit(solution)/shard_map/ppermute | solution.py:29
  49.5 24.2 %copy-start = (bf16[1,2,128,2048]{3,2,1,0:T(8,128)(2,1)}, bf16[1,2,128,2048]{3,2,1,0:T(8,128)(2,1)S(1)}, u32[]{:S(2)}) copy-start(bf16[1,2,128,2048]{3,2,1,0:T(8,128)(2,1)S(1)} %collective-permute-done.2) | copy-start | bytes 3145732
  89.3 2.3 %copy-start.1 = (bf16[1,2,128,2048]{3,2,1,0:T(8,128)(2,1)S(1)}, bf16[1,2,128,2048]{3,2,1,0:T(8,128)(2,1)}, u32[]{:S(2)}) copy-start(bf16[1,2,128,2048]{3,2,1,0:T(8,128)(2,1)} %copy-done) | copy-start | bytes 3145732
Sparse Core Ops, SparseCore 0:
  96.7 20.7 all-reduce.1
